TPU v7x, 128 devices: a whole 4x4x4 slice. The times are simulated.
128 devices in a mesh: tile: 16 (over x, z_lo, core), col: 8 (over y, z_hi).
Axes of the slice: x: 4, y: 4, z: 4 (z_hi: 2, z_lo: 2; z = z_hi * 2 + z_lo), core: 2. Of those that a mesh axis runs over, the one named last changes fastest.
Arguments:
- u_velocity: float32 [8192, 4096], P('tile', 'col'), may hold values from -12 to 12
- v_velocity: float32 [8192, 4096], P('tile', 'col'), may hold values from -12 to 12
- ocean_mask: int32 [64, 32], P('tile', 'col'), may hold values from 0 to 1, as said below
- tile_owner: int32 [64, 32], P('tile', 'col'), may hold values from 0 to 15, as said below
- lower_edge_quarter_turns: int32 [16], replicated, may hold values from 0 to 3
Outputs:
- library: float32 [16, 8, 16, 16, 1024], P('tile', 'col')
- gram: float32 [16, 16], replicated
Inputs may be any that keep to these rules, and one draw needn't show every extreme that they name: `ocean_mask`: in every column of devices (4 x 4 tile blocks), at least one device has only ocean tiles. `tile_owner`: among the ocean tiles of one device at most 1 share an owner; the ocean tiles of one column of devices are spread over its 16 owners so that the owners' counts differ by at most one. Land tiles carry an owner that is not used.
All inputs are finite; a program needn't handle non-finite values.
Results may differ from a plain program's by a relative error of at most 0.00014.
Values sent between devices are 32-bit elements; how exact they have to be, the bound alone decides.
No kernel may reach another device: no remote copies, remote signals or barrier semaphores. Data moves between devices by JAX's collectives and lax.ppermute only.
A program may use at most 192 MiB of HBM per device.

v0:
```python
import jax
import jax.numpy as jnp
from jax import lax
from jax.sharding import PartitionSpec as P

PASSES = 8
KAPPA = 0.2


def with_halo(cells, sides, width):
    for axis, dim in sides:
        count = lax.axis_size(axis)
        head = lax.slice_in_dim(cells, 0, width, axis=dim)
        tail = lax.slice_in_dim(cells, cells.shape[dim] - width, cells.shape[dim], axis=dim)
        cells = jnp.concatenate(
            [
                lax.ppermute(tail, axis, [(i, (i + 1) % count) for i in range(count)]),
                cells,
                lax.ppermute(head, axis, [((i + 1) % count, i) for i in range(count)]),
            ],
            axis=dim,
        )
    return cells


def quarter(first, second, turns):
    cosine = jnp.where(turns == 0, 1.0, jnp.where(turns == 2, -1.0, 0.0)).astype(first.dtype)
    sine = jnp.where(turns == 1, 1.0, jnp.where(turns == 3, -1.0, 0.0)).astype(first.dtype)
    return (cosine * first - sine * second, sine * first + cosine * second)


def turn_rims(padded, width, k_top, k_bottom):
    top_u, top_v = quarter(padded[0, :width], padded[1, :width], k_top)
    low_u, low_v = quarter(padded[0, -width:], padded[1, -width:], k_bottom)
    upper = jnp.stack([top_u, top_v])
    lower = jnp.stack([low_u, low_v])
    return jnp.concatenate([upper, padded[:, width:-width], lower], axis=1)


def relax(padded):
    centre = padded[:, 1:-1, 1:-1]
    beside_all = (
        padded[:, :-2, 1:-1] + padded[:, 2:, 1:-1] + padded[:, 1:-1, :-2] + padded[:, 1:-1, 2:]
    )
    return centre + KAPPA * (beside_all - 4.0 * centre)


def derive(padded):
    first = padded[..., 0, :, :]
    second = padded[..., 1, :, :]
    u_part = first[..., 1:-1, 1:-1]
    v_part = second[..., 1:-1, 1:-1]
    u_dx = (first[..., 1:-1, 2:] - first[..., 1:-1, :-2]) * 0.5
    u_dy = (first[..., 2:, 1:-1] - first[..., :-2, 1:-1]) * 0.5
    v_dx = (second[..., 1:-1, 2:] - second[..., 1:-1, :-2]) * 0.5
    v_dy = (second[..., 2:, 1:-1] - second[..., :-2, 1:-1]) * 0.5
    return jnp.stack([u_part, v_part, v_dx - u_dy, u_dy + v_dx, u_dx - v_dy], axis=-3)


def make_terms(base):
    u_part = base[..., 0, :]
    v_part = base[..., 1, :]
    vort = base[..., 2, :]
    strain = base[..., 3, :]
    stretch = base[..., 4, :]
    listed = [
        u_part,
        v_part,
        vort,
        strain,
        stretch,
        vort * vort,
        vort * strain,
        vort * stretch,
        strain * strain,
        stretch * stretch,
        strain * stretch,
        u_part * vort,
        v_part * vort,
        u_part * strain,
        v_part * stretch,
        u_part * v_part,
    ]
    return jnp.stack(listed, axis=-2)


def to_tiles(field, grid_x, grid_y, side):
    leading = field.shape[:-2]
    shaped = field.reshape(leading + (grid_x, side, grid_y, side))
    shaped = jnp.swapaxes(shaped, -3, -2)
    return shaped.reshape(leading + (grid_x * grid_y, side * side))


def per_device(u_velocity, v_velocity, ocean_mask, tile_owner, lower_edge_quarter_turns):
    rows_tile = lax.axis_size("tile")
    here = lax.axis_index("tile")
    k_top = lower_edge_quarter_turns[here]
    k_bottom = (4 - lower_edge_quarter_turns[(here + 1) % rows_tile]) % 4
    field = jnp.stack([u_velocity, v_velocity])
    for step in range(PASSES):
        padded = with_halo(field, (("tile", 1), ("col", 2)), 1)
        field = relax(turn_rims(padded, 1, k_top, k_bottom))
    fine_rows, fine_cols = u_velocity.shape
    coarse = field.reshape(2, fine_rows // 4, 4, fine_cols // 4, 4).mean(axis=(2, 4))
    coarse_pad = with_halo(coarse, (("tile", 1), ("col", 2)), 1)
    coarse_pad = turn_rims(coarse_pad, 1, k_top, k_bottom)
    grid_x, grid_y = ocean_mask.shape
    side = coarse.shape[1] // grid_x
    starting_tile_set = jnp.swapaxes(to_tiles(derive(coarse_pad), grid_x, grid_y, side), 0, 1)
    live = ocean_mask.reshape(-1) == 1
    owners = tile_owner.reshape(-1)
    tiles = live.shape[0]
    slots = tiles // rows_tile
    local = jnp.arange(tiles, dtype=jnp.int32)
    same = (owners[:, None] == owners[None, :]) & live[None, :] & (local[None, :] < local[:, None])
    slot = jnp.sum(same.astype(jnp.int32), axis=1)
    target = jnp.arange(rows_tile * slots, dtype=jnp.int32)
    chosen_terms = (
        live[None, :]
        & (owners[None, :] == target[:, None] // slots)
        & (slot[None, :] == target[:, None] % slots)
    ).astype(jnp.float32)
    library = make_terms(
        lax.all_to_all(
            jnp.einsum(
                "vh,hsd->vsd", chosen_terms, starting_tile_set, precision=lax.Precision.HIGHEST
            ),
            "tile",
            split_axis=0,
            concat_axis=0,
            tiled=True,
        )
    )
    part = jnp.einsum("pnc,pmc->nm", library, library, precision=lax.Precision.HIGHEST)
    gram = lax.psum(part, ("tile", "col")) / (fine_rows // 4 * (fine_cols // 4))
    return (library[None, None], gram)


def solution(mesh):
    in_specs = (P("tile", "col"), P("tile", "col"), P("tile", "col"), P("tile", "col"), P())
    out_specs = (P("tile", "col", None, None, None), P())
    return jax.shard_map(
        per_device, mesh=mesh, in_specs=in_specs, out_specs=out_specs, check_vma=False
    )
```

profile of v0, /device:TPU:1, one launch (start us, length us, event | category | flops | bytes accessed | tf_op | source)
XLA Modules:
  0.0 374.1 jit_solution(4603771623657914441)
XLA Ops:
  8.2 3.5 collective-permute-start.2
  21.4 6.4 %fusion.45 = f32[2,512,512]{2,1,0:T(8,128)S(1)} fusion(f32[2,514,1]{2,1,0:T(8,128)} %copy-done.15, f32[2,1,512]{2,1,0:T(1,128)S(1)} %collective-permute-done.1, f32[2,1,512]{2,1,0:T(1,128)S(1)} %collective-permute-done, f32[1,512,512]{2,1,0:T(8,128)S(1)} %bitcast.34, f32[1,512,512]{2,1,0:T(8,128)S(1)} %bitcast.28, f32[2,514,1]{2,1,0:T(8,128)} %copy-done.13, ...), kind=kLoop, calls=%fused_computation.129 | loop fusion | flops 10485760 | bytes 6324288 | tf_op jit(solution)/shard_map/add | solution.py:45
  34.3 4.6 %collective-permute-start.7 = (f32[2,514,1]{1,0,2:T(2,128)S(1)}, f32[2,514,1]{1,0,2:T(2,128)S(1)}, u32[]{:S(2)}, u32[]{:S(2)}) collective-permute-start(f32[2,514,1]{1,0,2:T(2,128)S(1)} %copy.209), channel_id=1, source_target_pairs={{1,0},{2,1},{3,2},{4,3},{5,4},{6,5},{7,6},{0,7},{9,8},{10,9},{11,1... | collective-permute-start | bytes 12344 | tf_op jit(solution)/shard_map/ppermute | solution.py:19
  44.0 8.1 %fusion.39 = f32[2,512,512]{2,1,0:T(8,128)S(1)} fusion(f32[2,512,512]{2,1,0:T(8,128)} %copy-done.9, f32[2,514,1]{2,1,0:T(8,128)S(1)} %copy-done.16, f32[2,1,512]{2,1,0:T(1,128)S(1)} %collective-permute-done.5, f32[2,1,512]{2,1,0:T(1,128)S(1)} %collective-permute-done.4, f32[2,514,1]{2,1,0:T(8,128)} %copy-done.14, f32[2,512,514]{2,1,0:T(8,128)S(1)} %slice.600, ...), kind=kLoop, calls=%fused_computation.113 | loop fusion | flops 8912896 | bytes 6324288 | tf_op jit(solution)/shard_map/add | solution.py:45
  59.6 3.8 %collective-permute-start.11 = (f32[2,514,1]{1,0,2:T(2,128)S(1)}, f32[2,514,1]{1,0,2:T(2,128)S(1)}, u32[]{:S(2)}, u32[]{:S(2)}) collective-permute-start(f32[2,514,1]{1,0,2:T(2,128)S(1)} %copy.215), channel_id=1, source_target_pairs={{1,0},{2,1},{3,2},{4,3},{5,4},{6,5},{7,6},{0,7},{9,8},{10,9},{11,1... | collective-permute-start | bytes 12344 | tf_op jit(solution)/shard_map/ppermute | solution.py:19
  66.1 5.0 %fusion.33 = f32[2,512,512]{2,1,0:T(8,128)S(1)} fusion(f32[2,512,512]{2,1,0:T(8,128)S(1)} %fusion.39, f32[2,514,1]{2,1,0:T(8,128)S(1)} %copy.217, f32[2,1,512]{2,1,0:T(1,128)S(1)} %collective-permute-done.9, f32[2,1,512]{2,1,0:T(1,128)S(1)} %collective-permute-done.8, f32[2,514,1]{2,1,0:T(8,128)S(1)} %copy.216, f32[2,512,514]{2,1,0:T(8,128)S(1)} %slice.603, ...), kind=kLoop, calls=%fused_computation.97 | loop fusion | flops 8912896 | bytes 6324288 | tf_op jit(solution)/shard_map/add | solution.py:45
  71.8 4.6 %collective-permute-start.13 = (f32[2,1,512]{2,1,0:T(1,128)S(1)}, f32[2,1,512]{2,1,0:T(1,128)S(1)}, u32[]{:S(2)}, u32[]{:S(2)}) collective-permute-start(f32[2,1,512]{2,1,0:T(1,128)S(1)} %get-tuple-element.85), channel_id=1, source_target_pairs={{8,0},{16,8},{24,16},{32,24},{40,32},{48,40},{56,48},{64,56},{72,6... | collective-permute-start | bytes 12296 | tf_op jit(solution)/shard_map/ppermute | solution.py:19
  79.9 3.6 collective-permute-start.15
  86.0 5.0 %fusion.27 = f32[2,512,512]{2,1,0:T(8,128)S(1)} fusion(f32[2,512,512]{2,1,0:T(8,128)S(1)} %copy-done.1, f32[2,514,1]{2,1,0:T(8,128)S(1)} %copy.223, f32[2,1,512]{2,1,0:T(1,128)S(1)} %collective-permute-done.13, f32[2,1,512]{2,1,0:T(1,128)S(1)} %collective-permute-done.12, f32[2,514,1]{2,1,0:T(8,128)S(1)} %copy.222, f32[2,512,514]{2,1,0:T(8,128)S(1)} %slice.606, ...), kind=kLoop, calls=%fused_computation.81 | loop fusion | flops 8912896 | bytes 6324288 | tf_op jit(solution)/shard_map/add | solution.py:45
  91.0 5.6 %collective-permute-start.17 = (f32[2,1,512]{2,1,0:T(1,128)S(1)}, f32[2,1,512]{2,1,0:T(1,128)S(1)}, u32[]{:S(2)}, u32[]{:S(2)}) collective-permute-start(f32[2,1,512]{2,1,0:T(1,128)S(1)} %get-tuple-element.83), channel_id=1, source_target_pairs={{8,0},{16,8},{24,16},{32,24},{40,32},{48,40},{56,48},{64,56},{72,6... | collective-permute-start | bytes 12296 | tf_op jit(solution)/shard_map/ppermute | solution.py:19
  106.4 5.0 %fusion.21 = f32[2,512,512]{2,1,0:T(8,128)S(1)} fusion(f32[2,512,512]{2,1,0:T(8,128)S(1)} %copy-done.3, f32[2,514,1]{2,1,0:T(8,128)S(1)} %copy.229, f32[2,1,512]{2,1,0:T(1,128)S(1)} %collective-permute-done.17, f32[2,1,512]{2,1,0:T(1,128)S(1)} %collective-permute-done.16, f32[2,514,1]{2,1,0:T(8,128)S(1)} %copy.228, f32[2,512,514]{2,1,0:T(8,128)S(1)} %slice.609, ...), kind=kLoop, calls=%fused_computation.65 | loop fusion | flops 8912896 | bytes 6324288 | tf_op jit(solution)/shard_map/add | solution.py:45
  111.5 5.8 %collective-permute-start.21 = (f32[2,1,512]{2,1,0:T(1,128)S(1)}, f32[2,1,512]{2,1,0:T(1,128)S(1)}, u32[]{:S(2)}, u32[]{:S(2)}) collective-permute-start(f32[2,1,512]{2,1,0:T(1,128)S(1)} %get-tuple-element.81), channel_id=1, source_target_pairs={{8,0},{16,8},{24,16},{32,24},{40,32},{48,40},{56,48},{64,56},{72,6... | collective-permute-start | bytes 12296 | tf_op jit(solution)/shard_map/ppermute | solution.py:19
  121.1 3.3 collective-permute-start.23
  127.2 5.0 %fusion.15 = f32[2,512,512]{2,1,0:T(8,128)S(1)} fusion(f32[2,512,512]{2,1,0:T(8,128)S(1)} %copy-done.5, f32[2,514,1]{2,1,0:T(8,128)S(1)} %copy.235, f32[2,1,512]{2,1,0:T(1,128)S(1)} %collective-permute-done.21, f32[2,1,512]{2,1,0:T(1,128)S(1)} %collective-permute-done.20, f32[2,514,1]{2,1,0:T(8,128)S(1)} %copy.234, f32[2,512,514]{2,1,0:T(8,128)S(1)} %slice.612, ...), kind=kLoop, calls=%fused_computation.49 | loop fusion | flops 8912896 | bytes 6324288 | tf_op jit(solution)/shard_map/add | solution.py:45
  132.3 5.8 %collective-permute-start.25 = (f32[2,1,512]{2,1,0:T(1,128)S(1)}, f32[2,1,512]{2,1,0:T(1,128)S(1)}, u32[]{:S(2)}, u32[]{:S(2)}) collective-permute-start(f32[2,1,512]{2,1,0:T(1,128)S(1)} %get-tuple-element.79), channel_id=1, source_target_pairs={{8,0},{16,8},{24,16},{32,24},{40,32},{48,40},{56,48},{64,56},{72,6... | collective-permute-start | bytes 12296 | tf_op jit(solution)/shard_map/ppermute | solution.py:19
  149.0 4.9 %fusion.9 = f32[2,512,512]{2,1,0:T(8,128)S(1)} fusion(f32[2,512,512]{2,1,0:T(8,128)S(1)} %copy-done.8, f32[2,514,1]{2,1,0:T(8,128)S(1)} %copy.241, f32[2,1,512]{2,1,0:T(1,128)S(1)} %collective-permute-done.25, f32[2,1,512]{2,1,0:T(1,128)S(1)} %collective-permute-done.24, f32[2,514,1]{2,1,0:T(8,128)S(1)} %copy.240, f32[2,512,514]{2,1,0:T(8,128)S(1)} %slice.615, ...), kind=kLoop, calls=%fused_computation.33 | loop fusion | flops 8912896 | bytes 6324288 | tf_op jit(solution)/shard_map/add | solution.py:45
  154.1 5.8 %collective-permute-start.29 = (f32[2,1,512]{2,1,0:T(1,128)S(1)}, f32[2,1,512]{2,1,0:T(1,128)S(1)}, u32[]{:S(2)}, u32[]{:S(2)}) collective-permute-start(f32[2,1,512]{2,1,0:T(1,128)S(1)} %get-tuple-element.77), channel_id=1, source_target_pairs={{8,0},{16,8},{24,16},{32,24},{40,32},{48,40},{56,48},{64,56},{72,6... | collective-permute-start | bytes 12296 | tf_op jit(solution)/shard_map/ppermute | solution.py:19
  169.6 5.9 %fusion.3 = f32[2,512,512]{2,1,0:T(8,128)} fusion(f32[2,512,512]{2,1,0:T(8,128)S(1)} %fusion.9, f32[2,514,1]{2,1,0:T(8,128)S(1)} %copy.247, f32[2,1,512]{2,1,0:T(1,128)S(1)} %collective-permute-done.29, f32[2,1,512]{2,1,0:T(1,128)S(1)} %collective-permute-done.28, f32[2,514,1]{2,1,0:T(8,128)S(1)} %copy.246, f32[2,512,514]{2,1,0:T(8,128)S(1)} %slice.618, ...), kind=kLoop, calls=%fused_computation.17 | loop fusion | flops 8912896 | bytes 6324288 | tf_op jit(solution)/shard_map/add | solution.py:45
  175.5 71.4 %reshape.326 = f32[2,128,4,128,4]{4,3,2,1,0:T(8,128)} reshape(f32[2,512,512]{2,1,0:T(8,128)} %fusion.3) | data formatting | bytes 4194304 | tf_op jit(solution)/shard_map/reshape | solution.py:104
  246.9 20.8 %reduce_sum.19 = f32[2,128,128]{2,1,0:T(8,128)S(1)} reduce(f32[2,128,4,128,4]{4,3,2,1,0:T(8,128)} %reshape.326, f32[]{:T(128)} %constant.89.clone.1), dimensions={2,4}, to_apply=%region_1.2 | reduce | flops 491520 | bytes 2228228 | tf_op jit(solution)/shard_map/reduce_sum | solution.py:104
  267.8 5.7 %collective-permute-start.33 = (f32[2,1,128]{2,1,0:T(1,128)S(1)}, f32[2,1,128]{2,1,0:T(1,128)S(1)}, u32[]{:S(2)}, u32[]{:S(2)}) collective-permute-start(f32[2,1,128]{2,1,0:T(1,128)S(1)} %get-tuple-element.113), channel_id=1, source_target_pairs={{8,0},{16,8},{24,16},{32,24},{40,32},{48,40},{56,48},{64,56},{72,6... | collective-permute-start | bytes 3080 | tf_op jit(solution)/shard_map/ppermute | solution.py:19
  274.4 4.0 %collective-permute-start.34 = (f32[2,130,1]{2,1,0:T(8,128)S(1)}, f32[2,130,1]{2,1,0:T(8,128)S(1)}, u32[]{:S(2)}, u32[]{:S(2)}) collective-permute-start(f32[2,130,1]{2,1,0:T(8,128)S(1)} %get-tuple-element.110), channel_id=1, source_target_pairs={{0,1},{1,2},{2,3},{3,4},{4,5},{5,6},{6,7},{7,0},{8,9},{9,10},{10,1... | collective-permute-start | bytes 3128 | tf_op jit(solution)/shard_map/ppermute | solution.py:17
  286.9 18.4 %all_to_all.5 = f32[16,5,1024]{2,1,0:T(8,128)S(1)} all-to-all(f32[16,5,1024]{2,1,0:T(8,128)S(1)} %copy.251), channel_id=1, replica_groups=mesh['tile'=16,'col'=8] {'tile'}, dimensions={0} | all-to-all | bytes 655360 | tf_op jit(solution)/shard_map/all_to_all | solution.py:124
  308.6 64.7 %psum.7 = f32[16,16]{1,0:T(8,128)S(1)} all-reduce(f32[16,16]{1,0:T(8,128)S(1)} %convolution_bitcast_fusion), channel_id=1, replica_groups=mesh['tile'=16,'col'=8] {'tile','col'}, use_global_device_ids=true, to_apply=%region_2.3 | all-reduce | flops 256 | bytes 2048 | tf_op jit(solution)/shard_map/psum | solution.py:135
  (234 shorter events, 92.4 us)
Async XLA Ops:
  8.2 10.1 %collective-permute-start.2 = (f32[2,514,1]{1,0,2:T(2,128)S(1)}, f32[2,514,1]{1,0,2:T(2,128)S(1)}, u32[]{:S(2)}, u32[]{:S(2)}) collective-permute-start(f32[2,514,1]{1,0,2:T(2,128)S(1)} %copy.202), channel_id=1, source_target_pairs={{0,1},{1,2},{2,3},{3,4},{4,5},{5,6},{6,7},{7,0},{8,9},{9,10},{10,1... | collective-permute-start | bytes 12344 | tf_op jit(solution)/shard_map/ppermute | solution.py:17
  12.0 6.6 %collective-permute-start.3 = (f32[2,514,1]{1,0,2:T(2,128)S(1)}, f32[2,514,1]{1,0,2:T(2,128)S(1)}, u32[]{:S(2)}, u32[]{:S(2)}) collective-permute-start(f32[2,514,1]{1,0,2:T(2,128)S(1)} %copy.203), channel_id=1, source_target_pairs={{1,0},{2,1},{3,2},{4,3},{5,4},{6,5},{7,6},{0,7},{9,8},{10,9},{11,1... | collective-permute-start | bytes 12344 | tf_op jit(solution)/shard_map/ppermute | solution.py:19
  33.3 6.1 %collective-permute-start.6 = (f32[2,514,1]{1,0,2:T(2,128)S(1)}, f32[2,514,1]{1,0,2:T(2,128)S(1)}, u32[]{:S(2)}, u32[]{:S(2)}) collective-permute-start(f32[2,514,1]{1,0,2:T(2,128)S(1)} %copy.208), channel_id=1, source_target_pairs={{0,1},{1,2},{2,3},{3,4},{4,5},{5,6},{6,7},{7,0},{8,9},{9,10},{10,1... | collective-permute-start | bytes 12344 | tf_op jit(solution)/shard_map/ppermute | solution.py:17
  34.3 5.4 %collective-permute-start.7 = (f32[2,514,1]{1,0,2:T(2,128)S(1)}, f32[2,514,1]{1,0,2:T(2,128)S(1)}, u32[]{:S(2)}, u32[]{:S(2)}) collective-permute-start(f32[2,514,1]{1,0,2:T(2,128)S(1)} %copy.209), channel_id=1, source_target_pairs={{1,0},{2,1},{3,2},{4,3},{5,4},{6,5},{7,6},{0,7},{9,8},{10,9},{11,1... | collective-permute-start | bytes 12344 | tf_op jit(solution)/shard_map/ppermute | solution.py:19
  57.6 6.6 %collective-permute-start.10 = (f32[2,514,1]{1,0,2:T(2,128)S(1)}, f32[2,514,1]{1,0,2:T(2,128)S(1)}, u32[]{:S(2)}, u32[]{:S(2)}) collective-permute-start(f32[2,514,1]{1,0,2:T(2,128)S(1)} %copy.214), channel_id=1, source_target_pairs={{0,1},{1,2},{2,3},{3,4},{4,5},{5,6},{6,7},{7,0},{8,9},{9,10},{10,1... | collective-permute-start | bytes 12344 | tf_op jit(solution)/shard_map/ppermute | solution.py:17
  71.1 5.9 %collective-permute-start.12 = (f32[2,1,512]{2,1,0:T(1,128)S(1)}, f32[2,1,512]{2,1,0:T(1,128)S(1)}, u32[]{:S(2)}, u32[]{:S(2)}) collective-permute-start(f32[2,1,512]{2,1,0:T(1,128)S(1)} %get-tuple-element.84), channel_id=1, source_target_pairs={{0,8},{8,16},{16,24},{24,32},{32,40},{40,48},{48,56},{56,64},{64,7... | collective-permute-start | bytes 12296 | tf_op jit(solution)/shard_map/ppermute | solution.py:17
  71.8 5.4 %collective-permute-start.13 = (f32[2,1,512]{2,1,0:T(1,128)S(1)}, f32[2,1,512]{2,1,0:T(1,128)S(1)}, u32[]{:S(2)}, u32[]{:S(2)}) collective-permute-start(f32[2,1,512]{2,1,0:T(1,128)S(1)} %get-tuple-element.85), channel_id=1, source_target_pairs={{8,0},{16,8},{24,16},{32,24},{40,32},{48,40},{56,48},{64,56},{72,6... | collective-permute-start | bytes 12296 | tf_op jit(solution)/shard_map/ppermute | solution.py:19
  77.7 6.4 %collective-permute-start.14 = (f32[2,514,1]{1,0,2:T(2,128)S(1)}, f32[2,514,1]{1,0,2:T(2,128)S(1)}, u32[]{:S(2)}, u32[]{:S(2)}) collective-permute-start(f32[2,514,1]{1,0,2:T(2,128)S(1)} %copy.220), channel_id=1, source_target_pairs={{0,1},{1,2},{2,3},{3,4},{4,5},{5,6},{6,7},{7,0},{8,9},{9,10},{10,1... | collective-permute-start | bytes 12344 | tf_op jit(solution)/shard_map/ppermute | solution.py:17
  90.9 6.3 %collective-permute-start.16 = (f32[2,1,512]{2,1,0:T(1,128)S(1)}, f32[2,1,512]{2,1,0:T(1,128)S(1)}, u32[]{:S(2)}, u32[]{:S(2)}) collective-permute-start(f32[2,1,512]{2,1,0:T(1,128)S(1)} %get-tuple-element.82), channel_id=1, source_target_pairs={{0,8},{8,16},{16,24},{24,32},{32,40},{40,48},{48,56},{56,64},{64,7... | collective-permute-start | bytes 12296 | tf_op jit(solution)/shard_map/ppermute | solution.py:17
  91.0 6.4 %collective-permute-start.17 = (f32[2,1,512]{2,1,0:T(1,128)S(1)}, f32[2,1,512]{2,1,0:T(1,128)S(1)}, u32[]{:S(2)}, u32[]{:S(2)}) collective-permute-start(f32[2,1,512]{2,1,0:T(1,128)S(1)} %get-tuple-element.83), channel_id=1, source_target_pairs={{8,0},{16,8},{24,16},{32,24},{40,32},{48,40},{56,48},{64,56},{72,6... | collective-permute-start | bytes 12296 | tf_op jit(solution)/shard_map/ppermute | solution.py:19
  97.9 6.3 %collective-permute-start.18 = (f32[2,514,1]{1,0,2:T(2,128)S(1)}, f32[2,514,1]{1,0,2:T(2,128)S(1)}, u32[]{:S(2)}, u32[]{:S(2)}) collective-permute-start(f32[2,514,1]{1,0,2:T(2,128)S(1)} %copy.226), channel_id=1, source_target_pairs={{0,1},{1,2},{2,3},{3,4},{4,5},{5,6},{6,7},{7,0},{8,9},{9,10},{10,1... | collective-permute-start | bytes 12344 | tf_op jit(solution)/shard_map/ppermute | solution.py:17
  111.4 6.4 %collective-permute-start.20 = (f32[2,1,512]{2,1,0:T(1,128)S(1)}, f32[2,1,512]{2,1,0:T(1,128)S(1)}, u32[]{:S(2)}, u32[]{:S(2)}) collective-permute-start(f32[2,1,512]{2,1,0:T(1,128)S(1)} %get-tuple-element.80), channel_id=1, source_target_pairs={{0,8},{8,16},{16,24},{24,32},{32,40},{40,48},{48,56},{56,64},{64,7... | collective-permute-start | bytes 12296 | tf_op jit(solution)/shard_map/ppermute | solution.py:17
  111.5 6.6 %collective-permute-start.21 = (f32[2,1,512]{2,1,0:T(1,128)S(1)}, f32[2,1,512]{2,1,0:T(1,128)S(1)}, u32[]{:S(2)}, u32[]{:S(2)}) collective-permute-start(f32[2,1,512]{2,1,0:T(1,128)S(1)} %get-tuple-element.81), channel_id=1, source_target_pairs={{8,0},{16,8},{24,16},{32,24},{40,32},{48,40},{56,48},{64,56},{72,6... | collective-permute-start | bytes 12296 | tf_op jit(solution)/shard_map/ppermute | solution.py:19
  118.6 6.1 %collective-permute-start.22 = (f32[2,514,1]{1,0,2:T(2,128)S(1)}, f32[2,514,1]{1,0,2:T(2,128)S(1)}, u32[]{:S(2)}, u32[]{:S(2)}) collective-permute-start(f32[2,514,1]{1,0,2:T(2,128)S(1)} %copy.232), channel_id=1, source_target_pairs={{0,1},{1,2},{2,3},{3,4},{4,5},{5,6},{6,7},{7,0},{8,9},{9,10},{10,1... | collective-permute-start | bytes 12344 | tf_op jit(solution)/shard_map/ppermute | solution.py:17
  132.2 6.4 %collective-permute-start.24 = (f32[2,1,512]{2,1,0:T(1,128)S(1)}, f32[2,1,512]{2,1,0:T(1,128)S(1)}, u32[]{:S(2)}, u32[]{:S(2)}) collective-permute-start(f32[2,1,512]{2,1,0:T(1,128)S(1)} %get-tuple-element.78), channel_id=1, source_target_pairs={{0,8},{8,16},{16,24},{24,32},{32,40},{40,48},{48,56},{56,64},{64,7... | collective-permute-start | bytes 12296 | tf_op jit(solution)/shard_map/ppermute | solution.py:17
  132.3 6.6 %collective-permute-start.25 = (f32[2,1,512]{2,1,0:T(1,128)S(1)}, f32[2,1,512]{2,1,0:T(1,128)S(1)}, u32[]{:S(2)}, u32[]{:S(2)}) collective-permute-start(f32[2,1,512]{2,1,0:T(1,128)S(1)} %get-tuple-element.79), channel_id=1, source_target_pairs={{8,0},{16,8},{24,16},{32,24},{40,32},{48,40},{56,48},{64,56},{72,6... | collective-permute-start | bytes 12296 | tf_op jit(solution)/shard_map/ppermute | solution.py:19
  139.3 6.1 %collective-permute-start.26 = (f32[2,514,1]{1,0,2:T(2,128)S(1)}, f32[2,514,1]{1,0,2:T(2,128)S(1)}, u32[]{:S(2)}, u32[]{:S(2)}) collective-permute-start(f32[2,514,1]{1,0,2:T(2,128)S(1)} %copy.238), channel_id=1, source_target_pairs={{0,1},{1,2},{2,3},{3,4},{4,5},{5,6},{6,7},{7,0},{8,9},{9,10},{10,1... | collective-permute-start | bytes 12344 | tf_op jit(solution)/shard_map/ppermute | solution.py:17
  154.0 6.4 %collective-permute-start.28 = (f32[2,1,512]{2,1,0:T(1,128)S(1)}, f32[2,1,512]{2,1,0:T(1,128)S(1)}, u32[]{:S(2)}, u32[]{:S(2)}) collective-permute-start(f32[2,1,512]{2,1,0:T(1,128)S(1)} %get-tuple-element.76), channel_id=1, source_target_pairs={{0,8},{8,16},{16,24},{24,32},{32,40},{40,48},{48,56},{56,64},{64,7... | collective-permute-start | bytes 12296 | tf_op jit(solution)/shard_map/ppermute | solution.py:17
  154.1 6.6 %collective-permute-start.29 = (f32[2,1,512]{2,1,0:T(1,128)S(1)}, f32[2,1,512]{2,1,0:T(1,128)S(1)}, u32[]{:S(2)}, u32[]{:S(2)}) collective-permute-start(f32[2,1,512]{2,1,0:T(1,128)S(1)} %get-tuple-element.77), channel_id=1, source_target_pairs={{8,0},{16,8},{24,16},{32,24},{40,32},{48,40},{56,48},{64,56},{72,6... | collective-permute-start | bytes 12296 | tf_op jit(solution)/shard_map/ppermute | solution.py:19
  161.1 6.1 %collective-permute-start.30 = (f32[2,514,1]{1,0,2:T(2,128)S(1)}, f32[2,514,1]{1,0,2:T(2,128)S(1)}, u32[]{:S(2)}, u32[]{:S(2)}) collective-permute-start(f32[2,514,1]{1,0,2:T(2,128)S(1)} %copy.244), channel_id=1, source_target_pairs={{0,1},{1,2},{2,3},{3,4},{4,5},{5,6},{6,7},{7,0},{8,9},{9,10},{10,1... | collective-permute-start | bytes 12344 | tf_op jit(solution)/shard_map/ppermute | solution.py:17
  267.7 6.3 %collective-permute-start.32 = (f32[2,1,128]{2,1,0:T(1,128)S(1)}, f32[2,1,128]{2,1,0:T(1,128)S(1)}, u32[]{:S(2)}, u32[]{:S(2)}) collective-permute-start(f32[2,1,128]{2,1,0:T(1,128)S(1)} %get-tuple-element.112), channel_id=1, source_target_pairs={{0,8},{8,16},{16,24},{24,32},{32,40},{40,48},{48,56},{56,64},{64,7... | collective-permute-start | bytes 3080 | tf_op jit(solution)/shard_map/ppermute | solution.py:17
  267.8 6.5 %collective-permute-start.33 = (f32[2,1,128]{2,1,0:T(1,128)S(1)}, f32[2,1,128]{2,1,0:T(1,128)S(1)}, u32[]{:S(2)}, u32[]{:S(2)}) collective-permute-start(f32[2,1,128]{2,1,0:T(1,128)S(1)} %get-tuple-element.113), channel_id=1, source_target_pairs={{8,0},{16,8},{24,16},{32,24},{40,32},{48,40},{56,48},{64,56},{72,6... | collective-permute-start | bytes 3080 | tf_op jit(solution)/shard_map/ppermute | solution.py:19
  274.4 7.6 %collective-permute-start.34 = (f32[2,130,1]{2,1,0:T(8,128)S(1)}, f32[2,130,1]{2,1,0:T(8,128)S(1)}, u32[]{:S(2)}, u32[]{:S(2)}) collective-permute-start(f32[2,130,1]{2,1,0:T(8,128)S(1)} %get-tuple-element.110), channel_id=1, source_target_pairs={{0,1},{1,2},{2,3},{3,4},{4,5},{5,6},{6,7},{7,0},{8,9},{9,10},{10,1... | collective-permute-start | bytes 3128 | tf_op jit(solution)/shard_map/ppermute | solution.py:17
  278.5 5.4 %collective-permute-start.35 = (f32[2,130,1]{2,1,0:T(8,128)S(1)}, f32[2,130,1]{2,1,0:T(8,128)S(1)}, u32[]{:S(2)}, u32[]{:S(2)}) collective-permute-start(f32[2,130,1]{2,1,0:T(8,128)S(1)} %get-tuple-element.111), channel_id=1, source_target_pairs={{1,0},{2,1},{3,2},{4,3},{5,4},{6,5},{7,6},{0,7},{9,8},{10,9},{11,1... | collective-permute-start | bytes 3128 | tf_op jit(solution)/shard_map/ppermute | solution.py:19
  (33 other events, 244.8 us)
where the time goes:
time: 381 us; the launch traced here: 374 us
  starting transfers between devices  91.9 us (24%)
  local copies, waits for them, and re-layouts  89.5 us (23%)
  blocking collectives  83.1 us (22%)
  other arithmetic  81.8 us (21%)
  waiting for transfers between devices  20.8 us (5%)
  between operations  5.18 us (1%)
    reshape x1, local copies, waits for them, and re-layouts, per_device(): field.reshape(2, fine_rows // 4, 4, fine_cols // 4, 4).mean(axis=(2, 4))  71.4 us
    psum x1, blocking collectives, per_device(): gram = lax.psum(part, ('tile', 'col')) / (fine_rows // 4 * (fine_cols // 4))  64.7 us
    ppermute x18, starting transfers between devices, with_halo(): lax.ppermute(head, axis, [((i + 1) % count, i) for i in range(count)])  64.6 us
    add x8, other arithmetic, relax(): return centre + KAPPA * (beside_all - 4.0 * centre)  45.1 us
    ppermute x18, starting transfers between devices, with_halo(): lax.ppermute(tail, axis, [(i, (i + 1) % count) for i in range(count)])  27.3 us
    reduce_sum x1, other arithmetic, per_device(): field.reshape(2, fine_rows // 4, 4, fine_cols // 4, 4).mean(axis=(2, 4))  20.8 us
    all_to_all x1, blocking collectives, per_device(): lax.all_to_all(jnp.einsum('vh,hsd->vsd', chosen_terms, starting_tile_set,...  18.4 us
    ppermute x18, waiting for transfers between devices, with_halo(): lax.ppermute(tail, axis, [(i, (i + 1) % count) for i in range(count)])  11.6 us
  transfers between devices with their start and end apart: 36, of which 31 were waited for; matrix products, arithmetic and copies ran while one was open for 1% of the time, Pallas kernels for 0%

commit v1 on v0

--- a/solution.py
+++ b/solution.py
@@ -5,6 +5,12 @@
 
 PASSES = 8
 KAPPA = 0.2
+
+
+def summed_here(shard, name):
+    parts = lax.all_gather(shard, name, axis=0, tiled=False)
+    total = parts.sum(axis=0)
+    return total
 
 
 def with_halo(cells, sides, width):
@@ -132,7 +138,7 @@
         )
     )
     part = jnp.einsum("pnc,pmc->nm", library, library, precision=lax.Precision.HIGHEST)
-    gram = lax.psum(part, ("tile", "col")) / (fine_rows // 4 * (fine_cols // 4))
+    gram = summed_here(part, ("tile", "col")) / (fine_rows // 4 * (fine_cols // 4))
     return (library[None, None], gram)
 
 

time: 381 us -> 636 us (1.67)
  the two profiles are of different devices: /device:TPU:1 before, /device:TPU:0 now
where the time goes in v1:
time: 636 us; the launch traced here: 629 us
  blocking collectives  334 us (53%)
  local copies, waits for them, and re-layouts  89.5 us (14%)
  starting transfers between devices  88.6 us (14%)
  other arithmetic  81.9 us (13%)
  waiting for transfers between devices  28.3 us (4%)
    all_gather x1, blocking collectives, summed_here(): parts = lax.all_gather(shard, name, axis=0, tiled=False)  320 us
    reshape x1, local copies, waits for them, and re-layouts, per_device(): field.reshape(2, fine_rows // 4, 4, fine_cols // 4, 4).mean(axis=(2, 4))  71.4 us
    ppermute x18, starting transfers between devices, with_halo(): lax.ppermute(head, axis, [((i + 1) % count, i) for i in range(count)])  63.5 us
    add x8, other arithmetic, relax(): return centre + KAPPA * (beside_all - 4.0 * centre)  45.1 us
    ppermute x18, starting transfers between devices, with_halo(): lax.ppermute(tail, axis, [(i, (i + 1) % count) for i in range(count)])  25.1 us
    ppermute x18, waiting for transfers between devices, with_halo(): lax.ppermute(tail, axis, [(i, (i + 1) % count) for i in range(count)])  22.6 us
    reduce_sum x1, other arithmetic, per_device(): field.reshape(2, fine_rows // 4, 4, fine_cols // 4, 4).mean(axis=(2, 4))  20.8 us
    all_to_all x1, blocking collectives, per_device(): lax.all_to_all(jnp.einsum('vh,hsd->vsd', chosen_terms, starting_tile_set,...  14.1 us
  transfers between devices with their start and end apart: 36, of which 23 were waited for; matrix products, arithmetic and copies ran while one was open for 1% of the time, Pallas kernels for 0%

profile of v1, /device:TPU:0, one launch (start us, length us, event | category | flops | bytes accessed | tf_op | source)
XLA Modules:
  0.0 629.1 jit_solution(9926816217170332945)
XLA Ops:
  1.7 3.8 collective-permute-start.1
  7.3 4.0 collective-permute-start.2
  20.9 6.4 %fusion.45 = f32[2,512,512]{2,1,0:T(8,128)S(1)} fusion(f32[2,514,1]{2,1,0:T(8,128)} %copy-done.15, f32[2,1,512]{2,1,0:T(1,128)S(1)} %collective-permute-done.1, f32[2,1,512]{2,1,0:T(1,128)S(1)} %collective-permute-done, f32[1,512,512]{2,1,0:T(8,128)S(1)} %bitcast.35, f32[1,512,512]{2,1,0:T(8,128)S(1)} %bitcast.29, f32[2,514,1]{2,1,0:T(8,128)} %copy-done.13, ...), kind=kLoop, calls=%fused_computation.129 | loop fusion | flops 10485760 | bytes 6324288 | tf_op jit(solution)/shard_map/add | solution.py:51
  27.4 3.8 collective-permute-start.5
  36.2 4.8 collective-permute-start.7
  46.7 8.1 %fusion.39 = f32[2,512,512]{2,1,0:T(8,128)S(1)} fusion(f32[2,512,512]{2,1,0:T(8,128)} %copy-done.9, f32[2,514,1]{2,1,0:T(8,128)S(1)} %copy-done.16, f32[2,1,512]{2,1,0:T(1,128)S(1)} %collective-permute-done.5, f32[2,1,512]{2,1,0:T(1,128)S(1)} %collective-permute-done.4, f32[2,514,1]{2,1,0:T(8,128)} %copy-done.14, f32[2,512,514]{2,1,0:T(8,128)S(1)} %slice.600, ...), kind=kLoop, calls=%fused_computation.113 | loop fusion | flops 8912896 | bytes 6324288 | tf_op jit(solution)/shard_map/add | solution.py:51
  54.9 3.8 collective-permute-start.9
  62.8 3.8 collective-permute-start.11
  69.9 5.0 fusion.33
  74.9 3.8 collective-permute-start.13
  90.1 5.0 fusion.27
  95.1 3.8 collective-permute-start.17
  110.7 5.0 fusion.21
  115.8 3.8 collective-permute-start.21
  131.5 5.0 fusion.15
  136.6 3.8 collective-permute-start.25
  153.3 4.9 fusion.9
  173.7 5.9 fusion.3
  179.7 71.4 %reshape.326 = f32[2,128,4,128,4]{4,3,2,1,0:T(8,128)} reshape(f32[2,512,512]{2,1,0:T(8,128)} %fusion.3) | data formatting | bytes 4194304 | tf_op jit(solution)/shard_map/reshape | solution.py:110
  251.1 20.8 %reduce_sum.28 = f32[2,128,128]{2,1,0:T(8,128)S(1)} reduce(f32[2,128,4,128,4]{4,3,2,1,0:T(8,128)} %reshape.326, f32[]{:T(128)} %constant.89.clone.1), dimensions={2,4}, to_apply=%region_1.2 | reduce | flops 491520 | bytes 2228228 | tf_op jit(solution)/shard_map/reduce_sum | solution.py:110
  272.0 3.8 collective-permute-start.33
  277.3 4.3 collective-permute-start.34
  291.1 14.1 %all_to_all.5 = f32[16,5,1024]{2,1,0:T(8,128)S(1)} all-to-all(f32[16,5,1024]{2,1,0:T(8,128)S(1)} %copy.251), channel_id=1, replica_groups=mesh['tile'=16,'col'=8] {'tile'}, dimensions={0} | all-to-all | bytes 655360 | tf_op jit(solution)/shard_map/all_to_all | solution.py:130
  308.5 319.6 %all-gather = f32[2048,16]{1,0:T(8,128)S(1)} all-gather(f32[16,16]{1,0:T(8,128)S(1)} %convolution_bitcast_fusion), channel_id=2, replica_groups=mesh['tile'=16,'col'=8] {'tile','col'}, dimensions={0}, use_global_device_ids=true | all-gather | bytes 132096 | tf_op jit(solution)/shard_map/all_gather | solution.py:11
  (235 shorter events, 105.2 us)
Async XLA Ops:
  7.3 10.6 %collective-permute-start.2 = (f32[2,514,1]{1,0,2:T(2,128)S(1)}, f32[2,514,1]{1,0,2:T(2,128)S(1)}, u32[]{:S(2)}, u32[]{:S(2)}) collective-permute-start(f32[2,514,1]{1,0,2:T(2,128)S(1)} %copy.202), channel_id=1, source_target_pairs={{0,1},{1,2},{2,3},{3,4},{4,5},{5,6},{6,7},{7,0},{8,9},{9,10},{10,1... | collective-permute-start | bytes 12344 | tf_op jit(solution)/shard_map/ppermute | solution.py:23
  11.5 6.6 %collective-permute-start.3 = (f32[2,514,1]{1,0,2:T(2,128)S(1)}, f32[2,514,1]{1,0,2:T(2,128)S(1)}, u32[]{:S(2)}, u32[]{:S(2)}) collective-permute-start(f32[2,514,1]{1,0,2:T(2,128)S(1)} %copy.203), channel_id=1, source_target_pairs={{1,0},{2,1},{3,2},{4,3},{5,4},{6,5},{7,6},{0,7},{9,8},{10,9},{11,1... | collective-permute-start | bytes 12344 | tf_op jit(solution)/shard_map/ppermute | solution.py:25
  27.3 5.2 collective-permute-start.4
  34.8 7.3 %collective-permute-start.6 = (f32[2,514,1]{1,0,2:T(2,128)S(1)}, f32[2,514,1]{1,0,2:T(2,128)S(1)}, u32[]{:S(2)}, u32[]{:S(2)}) collective-permute-start(f32[2,514,1]{1,0,2:T(2,128)S(1)} %copy.208), channel_id=1, source_target_pairs={{0,1},{1,2},{2,3},{3,4},{4,5},{5,6},{6,7},{7,0},{8,9},{9,10},{10,1... | collective-permute-start | bytes 12344 | tf_op jit(solution)/shard_map/ppermute | solution.py:23
  36.2 6.2 collective-permute-start.7
  54.8 5.2 collective-permute-start.8
  60.5 7.5 %collective-permute-start.10 = (f32[2,514,1]{1,0,2:T(2,128)S(1)}, f32[2,514,1]{1,0,2:T(2,128)S(1)}, u32[]{:S(2)}, u32[]{:S(2)}) collective-permute-start(f32[2,514,1]{1,0,2:T(2,128)S(1)} %copy.214), channel_id=1, source_target_pairs={{0,1},{1,2},{2,3},{3,4},{4,5},{5,6},{6,7},{7,0},{8,9},{9,10},{10,1... | collective-permute-start | bytes 12344 | tf_op jit(solution)/shard_map/ppermute | solution.py:23
  62.8 5.5 collective-permute-start.11
  74.8 5.2 collective-permute-start.12
  80.6 7.3 %collective-permute-start.14 = (f32[2,514,1]{1,0,2:T(2,128)S(1)}, f32[2,514,1]{1,0,2:T(2,128)S(1)}, u32[]{:S(2)}, u32[]{:S(2)}) collective-permute-start(f32[2,514,1]{1,0,2:T(2,128)S(1)} %copy.220), channel_id=1, source_target_pairs={{0,1},{1,2},{2,3},{3,4},{4,5},{5,6},{6,7},{7,0},{8,9},{9,10},{10,1... | collective-permute-start | bytes 12344 | tf_op jit(solution)/shard_map/ppermute | solution.py:23
  83.1 5.4 collective-permute-start.15
  95.1 5.2 collective-permute-start.16
  100.8 7.3 %collective-permute-start.18 = (f32[2,514,1]{1,0,2:T(2,128)S(1)}, f32[2,514,1]{1,0,2:T(2,128)S(1)}, u32[]{:S(2)}, u32[]{:S(2)}) collective-permute-start(f32[2,514,1]{1,0,2:T(2,128)S(1)} %copy.226), channel_id=1, source_target_pairs={{0,1},{1,2},{2,3},{3,4},{4,5},{5,6},{6,7},{7,0},{8,9},{9,10},{10,1... | collective-permute-start | bytes 12344 | tf_op jit(solution)/shard_map/ppermute | solution.py:23
  115.7 5.2 collective-permute-start.20
  121.4 7.3 %collective-permute-start.22 = (f32[2,514,1]{1,0,2:T(2,128)S(1)}, f32[2,514,1]{1,0,2:T(2,128)S(1)}, u32[]{:S(2)}, u32[]{:S(2)}) collective-permute-start(f32[2,514,1]{1,0,2:T(2,128)S(1)} %copy.232), channel_id=1, source_target_pairs={{0,1},{1,2},{2,3},{3,4},{4,5},{5,6},{6,7},{7,0},{8,9},{9,10},{10,1... | collective-permute-start | bytes 12344 | tf_op jit(solution)/shard_map/ppermute | solution.py:23
  124.2 5.6 collective-permute-start.23
  136.5 5.2 collective-permute-start.24
  142.2 7.3 %collective-permute-start.26 = (f32[2,514,1]{1,0,2:T(2,128)S(1)}, f32[2,514,1]{1,0,2:T(2,128)S(1)}, u32[]{:S(2)}, u32[]{:S(2)}) collective-permute-start(f32[2,514,1]{1,0,2:T(2,128)S(1)} %copy.238), channel_id=1, source_target_pairs={{0,1},{1,2},{2,3},{3,4},{4,5},{5,6},{6,7},{7,0},{8,9},{9,10},{10,1... | collective-permute-start | bytes 12344 | tf_op jit(solution)/shard_map/ppermute | solution.py:23
  158.3 5.2 collective-permute-start.28
  164.0 7.3 %collective-permute-start.30 = (f32[2,514,1]{1,0,2:T(2,128)S(1)}, f32[2,514,1]{1,0,2:T(2,128)S(1)}, u32[]{:S(2)}, u32[]{:S(2)}) collective-permute-start(f32[2,514,1]{1,0,2:T(2,128)S(1)} %copy.244), channel_id=1, source_target_pairs={{0,1},{1,2},{2,3},{3,4},{4,5},{5,6},{6,7},{7,0},{8,9},{9,10},{10,1... | collective-permute-start | bytes 12344 | tf_op jit(solution)/shard_map/ppermute | solution.py:23
  166.8 5.3 collective-permute-start.31
  271.9 5.3 collective-permute-start.32
  277.3 8.7 %collective-permute-start.34 = (f32[2,130,1]{2,1,0:T(8,128)S(1)}, f32[2,130,1]{2,1,0:T(8,128)S(1)}, u32[]{:S(2)}, u32[]{:S(2)}) collective-permute-start(f32[2,130,1]{2,1,0:T(8,128)S(1)} %get-tuple-element.110), channel_id=1, source_target_pairs={{0,1},{1,2},{2,3},{3,4},{4,5},{5,6},{6,7},{7,0},{8,9},{9,10},{10,1... | collective-permute-start | bytes 3128 | tf_op jit(solution)/shard_map/ppermute | solution.py:23
  281.6 6.6 %collective-permute-start.35 = (f32[2,130,1]{2,1,0:T(8,128)S(1)}, f32[2,130,1]{2,1,0:T(8,128)S(1)}, u32[]{:S(2)}, u32[]{:S(2)}) collective-permute-start(f32[2,130,1]{2,1,0:T(8,128)S(1)} %get-tuple-element.111), channel_id=1, source_target_pairs={{1,0},{2,1},{3,2},{4,3},{5,4},{6,5},{7,6},{0,7},{9,8},{10,9},{11,1... | collective-permute-start | bytes 3128 | tf_op jit(solution)/shard_map/ppermute | solution.py:25
  (33 other events, 517.5 us)
